TPU v7x, 256 devices: a whole 4x4x8 slice. The times are simulated.
256 devices in a mesh: seq: 32 (over x, y, core), head: 8 (over z).
Axes of the slice: x: 4, y: 4, z: 8, core: 2. Of those that a mesh axis runs over, the one named last changes fastest.
Arguments:
- queries: float32 [65536, 1024], P('seq', 'head'), may hold values from -600 to 600
- keys: float32 [65536, 1024], P('seq', 'head'), may hold values from -6 to 6
- values: float32 [65536, 1024], P('seq', 'head'), may hold values from -6 to 6
- proj_e: float32 [65536, 256], P(('seq', 'head')), may hold values from -0.0234375 to 0.0234375
- proj_f: float32 [65536, 256], P(('seq', 'head')), may hold values from -0.0234375 to 0.0234375
- grad_out: float32 [65536, 1024], P('seq', 'head'), may hold values from -6 to 6
Outputs:
- grad_queries: float32 [65536, 1024], P('seq', 'head')
- grad_keys: float32 [65536, 1024], P('seq', 'head')
- grad_values: float32 [65536, 1024], P('seq', 'head')
- grad_e: float32 [65536, 256], P(('seq', 'head'))
- grad_f: float32 [65536, 256], P(('seq', 'head'))
All inputs are finite; a program needn't handle non-finite values.
Results may differ from a plain program's by a relative error of at most 0.0003.
Values sent between devices are 32-bit elements; how exact they have to be, the bound alone decides.
No kernel may reach another device: no remote copies, remote signals or barrier semaphores. Data moves between devices by JAX's collectives and lax.ppermute only.
A program may use at most 64 MiB of HBM per device.

v0:
```python
import functools
import math

import jax
import jax.numpy as jnp
from jax import lax
from jax.experimental import pallas as pl
from jax.experimental.pallas import tpu as pltpu
from jax.sharding import PartitionSpec as P


HD = 64

F32 = jnp.float32
BF16 = jnp.bfloat16


def seq_perm(move):
    pairs = []
    for x in range(4):
        for y in range(4):
            for core in range(2):
                tx, ty, tc = move(x, y, core)
                pairs.append(((x * 4 + y) * 2 + core, ((tx % 4) * 4 + ty % 4) * 2 + tc))
    return pairs


CORE = seq_perm(lambda x, y, c: (x, y, 1 - c))


FIRST = [seq_perm(lambda x, y, c, k=k: (x, y + k, c) if c else (x + k, y, c)) for k in range(4)]
SECOND = [seq_perm(lambda x, y, c, k=k: (x + k, y, c) if c else (x, y + k, c)) for k in range(4)]


def sum_over_seq(first, second):
    even = lax.axis_index("seq") % 2 == 0
    mine = jnp.where(even, first, second)
    mine = mine + lax.ppermute(jnp.where(even, second, first), "seq", CORE)
    for ring in (FIRST, SECOND):
        one, two, three = (lax.ppermute(mine, "seq", ring[k]) for k in (1, 2, 3))
        mine = (mine + two) + (one + three)
    other = lax.ppermute(mine, "seq", CORE)
    return jnp.where(even, mine, other), jnp.where(even, other, mine)


def shift(x, perm):
    return lax.ppermute(x, "head", perm)


def rings(n):
    up = [(i, (i + 1) % n) for i in range(n)]
    down = [(i, (i - 1) % n) for i in range(n)]
    return up, down


def gather_blocks(own, other, n):
    up, down = rings(n)
    half = n // 2
    e, f = [own] + [None] * (n - 1), [other] + [None] * (n - 1)
    for step in range(1, half):
        e[step] = shift(e[step - 1], down)
        e[-step] = shift(e[(1 - step) % n], up)
        f[step] = shift(f[step - 1], down)
        f[-step] = shift(f[(1 - step) % n], up)
    e[half] = shift(e[half - 1], down)
    f[half] = shift(f[half + 1], up)
    return e, f


def scatter_blocks(terms_e, terms_f, n, beside):
    up, down = rings(n)
    half = n // 2
    e_up = shift(terms_e[half], up)
    f_down = shift(terms_f[half], down)
    e_down = shift(terms_e[half + 1], down)
    f_up = shift(terms_f[half - 1], up)
    done = []
    for step in range(2, half + 1):
        near, far = half + 1 - step, half - 1 + step
        e_up = shift(e_up + terms_e[near], up)
        f_down = shift(f_down + terms_f[far], down)
        if step < half:
            e_down = e_down + terms_e[far + 1]
            f_up = f_up + terms_f[near - 1]
            work = beside[len(done)]()
            f_up, work = lax.optimization_barrier((f_up, work))
            done.append(work)
            e_down = shift(e_down, down)
            f_up = shift(f_up, up)
    grad_e = (terms_e[0] + e_down) + e_up
    grad_f = (terms_f[0] + f_up) + f_down
    return grad_e, grad_f, done


def two(x):
    high = x.astype(BF16)
    return high, (x - high.astype(F32)).astype(BF16)


def three(x):
    high = x.astype(BF16)
    rest = x - high.astype(F32)
    mid = rest.astype(BF16)
    return high, mid, (rest - mid.astype(F32)).astype(BF16)


def move(to, source):
    rows = 32

    def step(i, carry):
        at = pl.ds(pl.multiple_of(i * rows, rows), rows)
        to[at, :] = source[at, :]
        return carry

    lax.fori_loop(0, source.shape[0] // rows, step, 0)


def mm(a, b):
    return lax.dot_general(a, b, (((1,), (0,)), ((), ())), preferred_element_type=F32)


VMEM = pl.BlockSpec(memory_space=pltpu.VMEM)
SMEM = pl.BlockSpec(memory_space=pltpu.SMEM)
LIMIT = 16 * 1024 * 1024


def call(body, out, n_in, scratch=(), flops=0, moved=0):
    single = not isinstance(out, tuple)
    return pl.pallas_call(
        body,
        out_shape=out,
        in_specs=[SMEM] + [VMEM] * n_in,
        out_specs=VMEM if single else tuple(VMEM for _ in out),
        scratch_shapes=list(scratch),
        compiler_params=pltpu.CompilerParams(vmem_limit_bytes=LIMIT),
        cost_estimate=pl.CostEstimate(flops=flops, bytes_accessed=moved, transcendentals=0),
    )


def six_pass(left_t, right):
    rows = left_t.shape[0]
    l1, l2, l3 = three(left_t)
    r1, r2, r3 = three(right)
    a = mm(jnp.concatenate([l1, l2, l3], axis=0), r1)
    b = mm(jnp.concatenate([l1, l2], axis=0), r2)
    c = mm(l1, r3)
    small = (a[2 * rows :] + b[rows:]) + c
    return (small + (a[rows : 2 * rows] + b[:rows])) + a[:rows]


def three_pass(left_t, right):
    rows = left_t.shape[0]
    l1, l2 = two(left_t)
    r1, r2 = two(right)
    a = mm(jnp.concatenate([l1, l2], axis=0), r1)
    return (a[rows:] + mm(l1, r2)) + a[:rows]


def partial_body(n, distances, z_ref, *refs):
    count = len(distances)
    es, fs = refs[:count], refs[count : 2 * count]
    keys, values = refs[2 * count : 2 * count + 2]
    pk_ref, pv_ref, e_stack, f_stack, e_buf, f_buf, came, went = refs[-8:]
    block = e_buf.shape[1]
    for j in range(count):
        pltpu.make_async_copy(es[j], e_buf.at[j], came.at[0, j]).start()
        pltpu.make_async_copy(fs[j], f_buf.at[j], came.at[1, j]).start()
    if len(refs) > 2 * count + 10:
        pk_ref[...] = refs[2 * count + 2][...]
        pv_ref[...] = refs[2 * count + 3][...]
    else:
        pk_ref[...] = jnp.zeros_like(pk_ref)
        pv_ref[...] = jnp.zeros_like(pv_ref)

    def out(i):
        d = jnp.int32(distances[0])
        for j, distance in enumerate(distances):
            d = jnp.where(i == j, distance, d)
        rows = pl.ds(pl.multiple_of(d * block, block), block)
        return d, (
            pltpu.make_async_copy(e_buf.at[i], e_stack.at[rows], went.at[0, i]),
            pltpu.make_async_copy(f_buf.at[i], f_stack.at[rows], went.at[1, i]),
        )

    def step(i, carry):
        d, copies = out(i)
        start = pl.multiple_of(lax.rem(z_ref[0] + d, n) * block, block)
        pltpu.make_async_copy(es[0], e_buf.at[i], came.at[0, i]).wait()
        pltpu.make_async_copy(fs[0], f_buf.at[i], came.at[1, i]).wait()
        for copy in copies:
            copy.start()
        pk_ref[...] += six_pass(keys[pl.ds(start, block), :].T, e_buf[i])
        pv_ref[...] += three_pass(values[pl.ds(start, block), :].T, f_buf[i])
        return carry

    lax.fori_loop(0, count, step, 0)

    def finish(i, carry):
        for copy in out(i)[1]:
            copy.wait()
        return carry

    lax.fori_loop(0, count, finish, 0)


def partial(n, z, distances, es, fs, keys, values, before=()):
    block, depth = es[0].shape
    width = keys.shape[1]
    count = len(distances)
    small = jax.ShapeDtypeStruct((width, depth), F32)
    stack = pltpu.HBM((n * block, depth), F32)
    anywhere = pl.BlockSpec(memory_space=pl.ANY)
    buffers = pltpu.VMEM((count, block, depth), F32)
    sems = pltpu.SemaphoreType.DMA((2, count))
    first = 2 * count + 3
    blocks = [
        which[d] if count == 1 else pltpu.with_memory_space_constraint(which[d], pltpu.HBM)
        for which in (es, fs)
        for d in distances
    ]
    return pl.pallas_call(
        functools.partial(partial_body, n, distances),
        out_shape=(small, small, stack, stack),
        in_specs=[SMEM] + [anywhere] * (2 * count) + [VMEM] * 2
        + ([VMEM, VMEM, anywhere, anywhere] if before else []),
        out_specs=(VMEM, VMEM, anywhere, anywhere),
        scratch_shapes=[buffers, buffers, sems, sems],
        input_output_aliases={first + 2: 2, first + 3: 3} if before else {},
        compiler_params=pltpu.CompilerParams(vmem_limit_bytes=LIMIT),
        cost_estimate=pl.CostEstimate(
            flops=10**8 * count, bytes_accessed=2**20 * count, transcendentals=0
        ),
    )(z, *blocks, keys, values, *before)


def middle_body(scale, q_ref, g_ref, pk_ref, pv_ref, gq_ref, gpk_ref, gpv_ref, ws, wt, wg, wq):
    heads = 2
    tile = q_ref.shape[0]
    width, depth = pk_ref.shape

    @pl.when(pl.program_id(0) == 0)
    def _():
        row = lax.broadcasted_iota(jnp.int32, (width, depth), 0)
        for h in range(heads):
            rows = slice(h * HD, (h + 1) * HD)
            p1, p2, p3 = three(pk_ref[rows, :])
            ws[h] = jnp.concatenate([p1, p2, p1, p1], axis=0)
            wt[h] = jnp.concatenate([p3, p2], axis=0)
            v1, v2 = two(pv_ref[rows, :])
            wg[h] = jnp.concatenate([v1, v2, v1, jnp.zeros_like(v1)], axis=0)
            own = (row >= h * HD) & (row < (h + 1) * HD)
            t1, t2 = two(jnp.where(own, pk_ref[...], 0.0).T)
            wq[h] = jnp.concatenate([t1, t2], axis=1)
        gpk_ref[...] = jnp.zeros_like(gpk_ref)
        gpv_ref[...] = jnp.zeros_like(gpv_ref)

    q = q_ref[...] * scale
    g = g_ref[...]
    qt1, qt2 = two(q.T)
    gt1, gt2 = two(g.T)
    left = lax.broadcasted_iota(jnp.int32, (tile, width), 1) < HD
    q_turned, g_turned = pltpu.roll(q, HD, 1), pltpu.roll(g, HD, 1)

    def doubled(x, turned, h):
        return jnp.where(left, turned, x) if h else jnp.where(left, x, turned)

    def products(h):
        x = doubled(q, q_turned, h)
        x1 = x.astype(BF16)
        rest = x - x1.astype(F32)
        last = rest - rest.astype(BF16).astype(F32)
        x23 = jnp.where(left, rest, last).astype(BF16)
        x12 = jnp.where(left, x, rest).astype(BF16)
        scores = mm(x12, wt[h]) + mm(jnp.concatenate([x1, x23], axis=1), ws[h])
        y = doubled(g, g_turned, h)
        y1 = y.astype(BF16)
        y2 = (y - y1.astype(F32)).astype(BF16)
        return scores, mm(jnp.concatenate([y1, y2], axis=1), wg[h])

    def softmax(scores, grad_probs):
        weights = jnp.exp(scores - jnp.max(scores, axis=-1, keepdims=True))
        inverse = 1.0 / jnp.sum(weights, axis=-1, keepdims=True)
        delta = jnp.sum(weights * grad_probs, axis=-1, keepdims=True) * inverse
        probs = weights * inverse
        return two(probs), two(probs * (grad_probs - delta))

    def gradients(h, probs, grad_scores):
        rows = slice(h * HD, (h + 1) * HD)
        p1, p2 = probs
        d1, d2 = grad_scores
        a = mm(jnp.concatenate([gt1[rows], gt2[rows]], axis=0), p1)
        gpv_ref[rows, :] += (a[HD:] + mm(gt1[rows], p2)) + a[:HD]
        a = mm(jnp.concatenate([qt1[rows], qt2[rows]], axis=0), d1)
        gpk_ref[rows, :] += (a[HD:] + mm(qt1[rows], d2)) + a[:HD]
        a = mm(d1, wq[h])
        return (a[:, width:] + mm(d2, wq[h, :, :width])) + a[:, :width]

    both = [products(h) for h in range(heads)]
    gq_ref[...] = sum(gradients(h, *softmax(*both[h])) for h in range(heads)) * scale


def middle(queries, grad_out, pk, pv, scale):
    count, width = queries.shape
    depth = pk.shape[1]
    tile = 512
    rows = pl.BlockSpec((tile, width), lambda i: (i, 0))
    whole = pl.BlockSpec((width, depth), lambda i: (0, 0))
    small = jax.ShapeDtypeStruct((width, depth), F32)
    return pl.pallas_call(
        functools.partial(middle_body, scale),
        grid=(count // tile,),
        out_shape=(jax.ShapeDtypeStruct((count, width), F32), small, small),
        in_specs=[rows, rows, whole, whole],
        out_specs=(rows, whole, whole),
        scratch_shapes=[
            pltpu.VMEM((2, 2 * width, depth), BF16),
            pltpu.VMEM((2, width, depth), BF16),
            pltpu.VMEM((2, 2 * width, depth), BF16),
            pltpu.VMEM((2, depth, 2 * width), BF16),
        ],
        compiler_params=pltpu.CompilerParams(
            vmem_limit_bytes=LIMIT, dimension_semantics=("arbitrary",)
        ),
        cost_estimate=pl.CostEstimate(flops=10**10, bytes_accessed=2**22, transcendentals=2**20),
        name="middle",
    )(queries, grad_out, pk, pv)


def term_of(rows, weights):
    r1, r2 = two(rows)
    w1, w2 = two(weights)
    both = mm(jnp.concatenate([r1, r2], axis=1), jnp.concatenate([w1, w1], axis=0))
    return mm(r1, w2) + both


def terms_body(n, e_at, f_at, z_ref, keys, values, gpk, gpv, *refs):
    *outs, e_now, f_now = refs
    block = outs[0].shape[0]
    count = len(e_at)

    def step(i, carry):
        e_d, f_d = jnp.int32(0), jnp.int32(0)
        for j in range(count):
            e_d = jnp.where(i == j, e_at[j], e_d)
            f_d = jnp.where(i == j, f_at[j], f_d)
        e_start = pl.multiple_of(lax.rem(z_ref[0] + e_d, n) * block, block)
        f_start = pl.multiple_of(lax.rem(z_ref[0] + f_d, n) * block, block)
        e_now[...] = term_of(keys[pl.ds(e_start, block), :], gpk[...])
        f_now[...] = term_of(values[pl.ds(f_start, block), :], gpv[...])
        for j in range(count):
            @pl.when(i == j)
            def _():
                move(outs[j], e_now)
                move(outs[count + j], f_now)
        return carry

    lax.fori_loop(0, count, step, 0)


def grads_body(z_ref, rows_ref, grads_ref, out_ref):
    width = grads_ref.shape[0]
    w1, w2 = two(grads_ref[...].T)
    r1, r2 = two(rows_ref[...])
    a = mm(r1, jnp.concatenate([w1, w2], axis=1))
    out_ref[...] = (a[:, width:] + mm(r2, w1)) + a[:, :width]


def products_of(z, stack, grads, n):
    width, depth = grads.shape
    block = stack.shape[0] // n
    return pl.pallas_call(
        grads_body,
        out_shape=jax.ShapeDtypeStruct((stack.shape[0], width), F32),
        grid_spec=pltpu.PrefetchScalarGridSpec(
            num_scalar_prefetch=1,
            grid=(n,),
            in_specs=[
                pl.BlockSpec((block, depth), lambda d, z_ref: (d, 0)),
                pl.BlockSpec((width, depth), lambda d, z_ref: (0, 0)),
            ],
            out_specs=pl.BlockSpec((block, width), lambda d, z_ref: (lax.rem(z_ref[0] + d, n), 0)),
        ),
        compiler_params=pltpu.CompilerParams(
            vmem_limit_bytes=LIMIT, dimension_semantics=("arbitrary",)
        ),
        cost_estimate=pl.CostEstimate(flops=10**9, bytes_accessed=2**22, transcendentals=0),
    )(z, stack, grads)


def whole(queries, keys, values, proj_e, proj_f, grad_out):
    scale = 1.0 / math.sqrt(HD)
    count, _ = queries.shape
    block, depth = proj_e.shape
    n = count // block
    z = lax.axis_index("head").astype(jnp.int32).reshape(1)
    square = jax.ShapeDtypeStruct((block, depth), F32)
    half = n // 2

    def run(body, out, *operands, scratch=(), flops=10**9):
        kernel = call(functools.partial(body, n), out, len(operands), scratch, flops, 2**22)
        return kernel(z, *operands)

    es, fs = gather_blocks(proj_e, proj_f, n)
    sums = ()
    for distances in (
        [d for d in range(n) if min(d, n - d) < half - 1], [half - 1, half + 1], [half]
    ):
        sums = partial(n, z, distances, es, fs, keys, values, sums)
    pk, pv, e_stack, f_stack = sums
    proj_keys, proj_vals = sum_over_seq(pk, pv)
    grad_query, gpk, gpv = middle(queries, grad_out, proj_keys, proj_vals, scale)
    gpk, gpv = sum_over_seq(gpk, gpv)
    terms_e, terms_f = [None] * n, [None] * n
    for e_at, f_at in (
        ([half, half + 1], [half, half - 1]),
        (
            [d for d in range(n) if d not in (half, half + 1)],
            [d for d in range(n) if d not in (half, half - 1)],
        ),
    ):
        blocks = run(
            lambda n, *refs, at=(e_at, f_at): terms_body(n, *at, *refs),
            (square,) * (len(e_at) + len(f_at)), keys, values, gpk, gpv,
            scratch=[pltpu.VMEM((block, depth), F32)] * 2,
        )
        for i, d in enumerate(e_at):
            terms_e[d] = blocks[i]
        for i, d in enumerate(f_at):
            terms_f[d] = blocks[len(e_at) + i]
    grad_e, grad_f, (grad_key, grad_value) = scatter_blocks(
        terms_e, terms_f, n,
        [lambda: products_of(z, e_stack, gpk, n), lambda: products_of(z, f_stack, gpv, n)],
    )
    return grad_query, grad_key, grad_value, grad_e, grad_f


def solution(mesh):
    tokens = P("seq", "head")
    rows = P(("seq", "head"), None)
    return jax.shard_map(
        whole,
        mesh=mesh,
        in_specs=(tokens, tokens, tokens, rows, rows, tokens),
        out_specs=(tokens, tokens, tokens, rows, rows),
        check_vma=False,
    )
```

profile of v0, /device:TPU:6, one launch (start us, length us, event | category | flops | bytes accessed | tf_op | source)
XLA Modules:
  0.0 149.1 jit_solution(11434347026303433123)
XLA Ops:
  0.6 5.9 %collective-permute-start = (f32[256,256]{1,0:T(8,128)}, f32[256,256]{1,0:T(8,128)S(1)}, u32[]{:S(2)}, u32[]{:S(2)}) collective-permute-start(f32[256,256]{1,0:T(8,128)} %refs_0_.1), channel_id=1, source_target_pairs={{0,7},{1,0},{2,1},{3,2},{4,3},{5,4},{6,5},{7,6},{8,15},{9,8},{10,9... | collective-permute-start | bytes 786440 | tf_op jit(solution)/shard_map/ppermute | solution.py:47
  6.6 3.3 %collective-permute-start.11 = (f32[256,256]{1,0:T(8,128)}, f32[256,256]{1,0:T(8,128)S(1)}, u32[]{:S(2)}, u32[]{:S(2)}) collective-permute-start(f32[256,256]{1,0:T(8,128)} %refs_5_.2), channel_id=1, source_target_pairs={{0,7},{1,0},{2,1},{3,2},{4,3},{5,4},{6,5},{7,6},{8,15},{9,8},{10,9... | collective-permute-start | bytes 786440 | tf_op jit(solution)/shard_map/ppermute | solution.py:47
  9.8 3.7 %collective-permute-done.refs_1_ = f32[256,256]{1,0:T(8,128)S(1)} collective-permute-done((f32[256,256]{1,0:T(8,128)}, f32[256,256]{1,0:T(8,128)S(1)}, u32[]{:S(2)}, u32[]{:S(2)}) %collective-permute-start) | collective-permute-done | bytes 262176 | tf_op jit(solution)/shard_map/ppermute | solution.py:47
  13.6 3.6 %collective-permute-start.1 = (f32[256,256]{1,0:T(8,128)S(1)}, f32[256,256]{1,0:T(8,128)S(1)}, u32[]{:S(2)}, u32[]{:S(2)}) collective-permute-start(f32[256,256]{1,0:T(8,128)S(1)} %collective-permute-done.refs_1_), channel_id=1, source_target_pairs={{0,7},{1,0},{2,1},{3,2},{4,3},{5,4},{6,5},{7,6},{8,15},{9,8},{10,9... | collective-permute-start | bytes 786440 | tf_op jit(solution)/shard_map/ppermute | solution.py:47
  17.2 5.6 %collective-permute-done.8.refs_4_ = f32[256,256]{1,0:T(8,128)S(1)} collective-permute-done((f32[256,256]{1,0:T(8,128)}, f32[256,256]{1,0:T(8,128)S(1)}, u32[]{:S(2)}, u32[]{:S(2)}) %collective-permute-start.8) | collective-permute-done | bytes 262176 | tf_op jit(solution)/shard_map/ppermute | solution.py:47
  22.8 3.2 %collective-permute-start.12 = (f32[256,256]{1,0:T(8,128)S(1)}, f32[256,256]{1,0:T(8,128)S(1)}, u32[]{:S(2)}, u32[]{:S(2)}) collective-permute-start(f32[256,256]{1,0:T(8,128)S(1)} %collective-permute-done.11.refs_6_), channel_id=1, source_target_pairs={{0,7},{1,0},{2,1},{3,2},{4,3},{5,4},{6,5},{7,6},{8,15},{9,8},{10,9... | collective-permute-start | bytes 786440 | tf_op jit(solution)/shard_map/ppermute | solution.py:47
  28.4 5.6 %collective-permute-done.9.refs_3_ = f32[256,256]{1,0:T(8,128)S(1)} collective-permute-done((f32[256,256]{1,0:T(8,128)S(1)}, f32[256,256]{1,0:T(8,128)S(1)}, u32[]{:S(2)}, u32[]{:S(2)}) %collective-permute-start.9) | collective-permute-done | bytes 262176 | tf_op jit(solution)/shard_map/ppermute | solution.py:47
  34.0 3.2 %collective-permute-start.13 = (f32[256,256]{1,0:T(8,128)S(1)}, f32[256,256]{1,0:T(8,128)}, u32[]{:S(2)}, u32[]{:S(2)}) collective-permute-start(f32[256,256]{1,0:T(8,128)S(1)} %collective-permute-done.12.refs_7_), channel_id=1, source_target_pairs={{0,7},{1,0},{2,1},{3,2},{4,3},{5,4},{6,5},{7,6},{8,15},{9,8},{10,9... | collective-permute-start | bytes 786440 | tf_op jit(solution)/shard_map/ppermute | solution.py:47
  42.2 3.5 %shard_map.101 = (f32[128,256]{1,0:T(8,128)S(1)}, f32[128,256]{1,0:T(8,128)S(1)}, f32[2048,256]{1,0:T(8,128)}, f32[2048,256]{1,0:T(8,128)}) custom-call(s32[1]{0:T(128)} %bitcast.z_ref.refs_0_, f32[256,256]{1,0:T(8,128)} %refs_0_.1, f32[256,256]{1,0:T(8,128)} %copy-done.8, f32[256,256]{1,0:T(8,128)} %copy-done.12, f32[256,256]{1,0:T(8,128)} %copy-done.16, ...), custom_call_target="tpu_custom_call" | custom-call | flops 500000000 | bytes 5242880 | tf_op jit(solution)/shard_map/pallas_call | solution.py:221
  46.5 2.3 %shard_map.102 = (f32[128,256]{1,0:T(8,128)S(1)}, f32[128,256]{1,0:T(8,128)S(1)}, f32[2048,256]{1,0:T(8,128)}, f32[2048,256]{1,0:T(8,128)}) custom-call(s32[1]{0:T(128)} %bitcast.z_ref.refs_0_, f32[256,256]{1,0:T(8,128)} %copy-done.14, f32[256,256]{1,0:T(8,128)} %copy-done.18, ...), custom_call_target="tpu_custom_call", output_to_operand_aliasing={{2}: (9, {}), {3}: (10, {})} | custom-call | flops 200000000 | bytes 2097152 | tf_op jit(solution)/shard_map/pallas_call | solution.py:221
  53.5 2.1 %collective-permute-start.16 = (f32[128,256]{1,0:T(8,128)S(1)}, f32[128,256]{1,0:T(8,128)S(1)}, u32[]{:S(2)}, u32[]{:S(2)}) collective-permute-start(f32[128,256]{1,0:T(8,128)S(1)} %select_add_fusion.1), channel_id=1, source_target_pairs={{0,64},{8,24},{16,80},{24,40},{32,96},{40,56},{48,112},{56,8},{64,... | collective-permute-start | bytes 393224 | tf_op jit(solution)/shard_map/ppermute | solution.py:40
  55.6 3.0 %collective-permute-done.15 = f32[128,256]{1,0:T(8,128)S(1)} collective-permute-done((f32[128,256]{1,0:T(8,128)S(1)}, f32[128,256]{1,0:T(8,128)S(1)}, u32[]{:S(2)}, u32[]{:S(2)}) %collective-permute-start.15) | collective-permute-done | bytes 131104 | tf_op jit(solution)/shard_map/ppermute | solution.py:40
  58.6 3.2 %collective-permute-done.17 = f32[128,256]{1,0:T(8,128)S(1)} collective-permute-done((f32[128,256]{1,0:T(8,128)S(1)}, f32[128,256]{1,0:T(8,128)S(1)}, u32[]{:S(2)}, u32[]{:S(2)}) %collective-permute-start.17) | collective-permute-done | bytes 131104 | tf_op jit(solution)/shard_map/ppermute | solution.py:40
  61.8 3.3 %collective-permute-start.18 = (f32[128,256]{1,0:T(8,128)S(1)}, f32[128,256]{1,0:T(8,128)S(1)}, u32[]{:S(2)}, u32[]{:S(2)}) collective-permute-start(f32[128,256]{1,0:T(8,128)S(1)} %add_add_fusion.5), channel_id=1, source_target_pairs={{0,32},{8,136},{16,48},{24,152},{32,0},{40,168},{48,16},{56,184},{... | collective-permute-start | bytes 393224 | tf_op jit(solution)/shard_map/ppermute | solution.py:40
  65.8 2.6 %collective-permute-start.20 = (f32[128,256]{1,0:T(8,128)S(1)}, f32[128,256]{1,0:T(8,128)S(1)}, u32[]{:S(2)}, u32[]{:S(2)}) collective-permute-start(f32[128,256]{1,0:T(8,128)S(1)} %add_add_fusion.5), channel_id=1, source_target_pairs={{0,48},{8,200},{16,0},{24,216},{32,16},{40,232},{48,32},{56,248},{... | collective-permute-start | bytes 393224 | tf_op jit(solution)/shard_map/ppermute | solution.py:40
  68.4 2.9 %collective-permute-done.19 = f32[128,256]{1,0:T(8,128)S(1)} collective-permute-done((f32[128,256]{1,0:T(8,128)S(1)}, f32[128,256]{1,0:T(8,128)S(1)}, u32[]{:S(2)}, u32[]{:S(2)}) %collective-permute-start.19) | collective-permute-done | bytes 131104 | tf_op jit(solution)/shard_map/ppermute | solution.py:40
  72.8 7.1 %middle.1 = (f32[2048,128]{1,0:T(8,128)}, f32[128,256]{1,0:T(8,128)S(1)}, f32[128,256]{1,0:T(8,128)S(1)}) custom-call(f32[2048,128]{1,0:T(8,128)S(1)} %copy-done.6, f32[2048,128]{1,0:T(8,128)S(1)} %copy-done.7, f32[128,256]{1,0:T(8,128)S(1)} %get-tuple-element.78.pk_ref, f32[128,256]{1,0:T(8,128)S(1)} %get-tuple-element.77.pv_ref), custom_call_target="tpu_custom_call" | custom-call | flops 10000000000 | bytes 4194304 | tf_op jit(solution)/shard_map/middle/pallas_call | solution.py:309
  83.6 4.4 %collective-permute-done.23 = f32[128,256]{1,0:T(8,128)S(1)} collective-permute-done((f32[128,256]{1,0:T(8,128)S(1)}, f32[128,256]{1,0:T(8,128)S(1)}, u32[]{:S(2)}, u32[]{:S(2)}) %collective-permute-start.23) | collective-permute-done | bytes 131104 | tf_op jit(solution)/shard_map/ppermute | solution.py:40
  90.9 2.6 %collective-permute-start.27 = (f32[128,256]{1,0:T(8,128)S(1)}, f32[128,256]{1,0:T(8,128)S(1)}, u32[]{:S(2)}, u32[]{:S(2)}) collective-permute-start(f32[128,256]{1,0:T(8,128)S(1)} %add_add_fusion.3), channel_id=1, source_target_pairs={{0,16},{8,72},{16,32},{24,88},{32,48},{40,104},{48,0},{56,120},{64... | collective-permute-start | bytes 393224 | tf_op jit(solution)/shard_map/ppermute | solution.py:40
  101.1 2.6 %collective-permute-start.40 = (f32[256,256]{1,0:T(8,128)S(1)}, f32[256,256]{1,0:T(8,128)S(1)}, u32[]{:S(2)}, u32[]{:S(2)}) collective-permute-start(f32[256,256]{1,0:T(8,128)S(1)} %get-tuple-element.71), channel_id=1, source_target_pairs={{0,7},{1,0},{2,1},{3,2},{4,3},{5,4},{6,5},{7,6},{8,15},{9,8},{10,9... | collective-permute-start | bytes 786440 | tf_op jit(solution)/shard_map/ppermute | solution.py:47
  103.7 2.6 %shard_map.105 = (f32[256,256]{1,0:T(8,128)S(1)}, f32[256,256]{1,0:T(8,128)S(1)}, f32[256,256]{1,0:T(8,128)S(1)}, f32[256,256]{1,0:T(8,128)S(1)}, f32[256,256]{1...) custom-call(s32[1]{0:T(128)} %bitcast.z_ref.refs_0_, ...), custom_call_target="tpu_custom_call" | custom-call | flops 1000000000 | bytes 4194304 | tf_op jit(solution)/shard_map/pallas_call | solution.py:401
  106.3 3.3 %collective-permute-done.40 = f32[256,256]{1,0:T(8,128)S(1)} collective-permute-done((f32[256,256]{1,0:T(8,128)S(1)}, f32[256,256]{1,0:T(8,128)S(1)}, u32[]{:S(2)}, u32[]{:S(2)}) %collective-permute-start.40) | collective-permute-done | bytes 262176 | tf_op jit(solution)/shard_map/ppermute | solution.py:47
  109.6 3.8 %collective-permute-start.41 = (f32[256,256]{1,0:T(8,128)S(1)}, f32[256,256]{1,0:T(8,128)S(1)}, u32[]{:S(2)}, u32[]{:S(2)}) collective-permute-start(f32[256,256]{1,0:T(8,128)S(1)} %add.114), channel_id=1, source_target_pairs={{0,7},{1,0},{2,1},{3,2},{4,3},{5,4},{6,5},{7,6},{8,15},{9,8},{10,9... | collective-permute-start | bytes 786440 | tf_op jit(solution)/shard_map/ppermute | solution.py:47
  115.5 4.2 %shard_map.106 = f32[2048,128]{1,0:T(8,128)} custom-call(s32[1]{0:T(128)} %bitcast.z_ref.refs_0_, f32[2048,256]{1,0:T(8,128)S(1)} %copy-done.4, f32[128,256]{1,0:T(8,128)S(1)} %get-tuple-element.76.refs_3_.grads_ref), custom_call_target="tpu_custom_call" | custom-call | flops 1000000000 | bytes 4194304 | tf_op jit(solution)/shard_map/pallas_call | solution.py:371
  120.1 3.8 %collective-permute-start.42 = (f32[256,256]{1,0:T(8,128)S(1)}, f32[256,256]{1,0:T(8,128)S(1)}, u32[]{:S(2)}, u32[]{:S(2)}) collective-permute-start(f32[256,256]{1,0:T(8,128)S(1)} %add.115), channel_id=1, source_target_pairs={{0,7},{1,0},{2,1},{3,2},{4,3},{5,4},{6,5},{7,6},{8,15},{9,8},{10,9... | collective-permute-start | bytes 786440 | tf_op jit(solution)/shard_map/ppermute | solution.py:47
  123.9 1.8 %collective-permute-done.32 = f32[256,256]{1,0:T(8,128)S(1)} collective-permute-done((f32[256,256]{1,0:T(8,128)S(1)}, f32[256,256]{1,0:T(8,128)S(1)}, u32[]{:S(2)}, u32[]{:S(2)}) %collective-permute-start.32) | collective-permute-done | bytes 262176 | tf_op jit(solution)/shard_map/ppermute | solution.py:47
  125.7 3.8 %collective-permute-start.33 = (f32[256,256]{1,0:T(8,128)S(1)}, f32[256,256]{1,0:T(8,128)S(1)}, u32[]{:S(2)}, u32[]{:S(2)}) collective-permute-start(f32[256,256]{1,0:T(8,128)S(1)} %add.106), channel_id=1, source_target_pairs={{0,7},{1,0},{2,1},{3,2},{4,3},{5,4},{6,5},{7,6},{8,15},{9,8},{10,9... | collective-permute-start | bytes 786440 | tf_op jit(solution)/shard_map/ppermute | solution.py:47
  129.6 4.2 %shard_map.107 = f32[2048,128]{1,0:T(8,128)} custom-call(s32[1]{0:T(128)} %bitcast.z_ref.refs_0_, f32[2048,256]{1,0:T(8,128)S(1)} %copy-done.5, f32[128,256]{1,0:T(8,128)S(1)} %get-tuple-element.75.refs_4_.grads_ref), custom_call_target="tpu_custom_call" | custom-call | flops 1000000000 | bytes 4194304 | tf_op jit(solution)/shard_map/pallas_call | solution.py:371
  134.1 3.3 %collective-permute-start.43 = (f32[256,256]{1,0:T(8,128)S(1)}, f32[256,256]{1,0:T(8,128)S(1)}, u32[]{:S(2)}, u32[]{:S(2)}) collective-permute-start(f32[256,256]{1,0:T(8,128)S(1)} %add.116), channel_id=1, source_target_pairs={{0,7},{1,0},{2,1},{3,2},{4,3},{5,4},{6,5},{7,6},{8,15},{9,8},{10,9... | collective-permute-start | bytes 786440 | tf_op jit(solution)/shard_map/ppermute | solution.py:47
  137.4 3.3 %collective-permute-start.34 = (f32[256,256]{1,0:T(8,128)S(1)}, f32[256,256]{1,0:T(8,128)S(1)}, u32[]{:S(2)}, u32[]{:S(2)}) collective-permute-start(f32[256,256]{1,0:T(8,128)S(1)} %add.107), channel_id=1, source_target_pairs={{0,7},{1,0},{2,1},{3,2},{4,3},{5,4},{6,5},{7,6},{8,15},{9,8},{10,9... | collective-permute-start | bytes 786440 | tf_op jit(solution)/shard_map/ppermute | solution.py:47
  140.8 3.5 %collective-permute-done.39 = f32[256,256]{1,0:T(8,128)S(1)} collective-permute-done((f32[256,256]{1,0:T(8,128)S(1)}, f32[256,256]{1,0:T(8,128)S(1)}, u32[]{:S(2)}, u32[]{:S(2)}) %collective-permute-start.39) | collective-permute-done | bytes 262176 | tf_op jit(solution)/shard_map/ppermute | solution.py:47
  146.5 1.9 %collective-permute-done.38 = f32[256,256]{1,0:T(8,128)S(1)} collective-permute-done((f32[256,256]{1,0:T(8,128)S(1)}, f32[256,256]{1,0:T(8,128)S(1)}, u32[]{:S(2)}, u32[]{:S(2)}) %collective-permute-start.38) | collective-permute-done | bytes 262176 | tf_op jit(solution)/shard_map/ppermute | solution.py:47
  (124 shorter events, 35.0 us)
Async XLA Ops:
  0.6 12.9 %collective-permute-start = (f32[256,256]{1,0:T(8,128)}, f32[256,256]{1,0:T(8,128)S(1)}, u32[]{:S(2)}, u32[]{:S(2)}) collective-permute-start(f32[256,256]{1,0:T(8,128)} %refs_0_.1), channel_id=1, source_target_pairs={{0,7},{1,0},{2,1},{3,2},{4,3},{5,4},{6,5},{7,6},{8,15},{9,8},{10,9... | collective-permute-start | bytes 786440 | tf_op jit(solution)/shard_map/ppermute | solution.py:47
  6.6 10.6 %collective-permute-start.4 = (f32[256,256]{1,0:T(8,128)}, f32[256,256]{1,0:T(8,128)S(1)}, u32[]{:S(2)}, u32[]{:S(2)}) collective-permute-start(f32[256,256]{1,0:T(8,128)} %refs_5_.2), channel_id=1, source_target_pairs={{0,1},{1,2},{2,3},{3,4},{4,5},{5,6},{6,7},{7,0},{8,9},{9,10},{10,1... | collective-permute-start | bytes 786440 | tf_op jit(solution)/shard_map/ppermute | solution.py:47
  6.6 16.2 %collective-permute-start.8 = (f32[256,256]{1,0:T(8,128)}, f32[256,256]{1,0:T(8,128)S(1)}, u32[]{:S(2)}, u32[]{:S(2)}) collective-permute-start(f32[256,256]{1,0:T(8,128)} %refs_0_.1), channel_id=1, source_target_pairs={{0,1},{1,2},{2,3},{3,4},{4,5},{5,6},{6,7},{7,0},{8,9},{9,10},{10,1... | collective-permute-start | bytes 786440 | tf_op jit(solution)/shard_map/ppermute | solution.py:47
  6.6 16.2 %collective-permute-start.11 = (f32[256,256]{1,0:T(8,128)}, f32[256,256]{1,0:T(8,128)S(1)}, u32[]{:S(2)}, u32[]{:S(2)}) collective-permute-start(f32[256,256]{1,0:T(8,128)} %refs_5_.2), channel_id=1, source_target_pairs={{0,7},{1,0},{2,1},{3,2},{4,3},{5,4},{6,5},{7,6},{8,15},{9,8},{10,9... | collective-permute-start | bytes 786440 | tf_op jit(solution)/shard_map/ppermute | solution.py:47
  13.6 12.5 %collective-permute-start.1 = (f32[256,256]{1,0:T(8,128)S(1)}, f32[256,256]{1,0:T(8,128)S(1)}, u32[]{:S(2)}, u32[]{:S(2)}) collective-permute-start(f32[256,256]{1,0:T(8,128)S(1)} %collective-permute-done.refs_1_), channel_id=1, source_target_pairs={{0,7},{1,0},{2,1},{3,2},{4,3},{5,4},{6,5},{7,6},{8,15},{9,8},{10,9... | collective-permute-start | bytes 786440 | tf_op jit(solution)/shard_map/ppermute | solution.py:47
  17.2 11.2 %collective-permute-start.5 = (f32[256,256]{1,0:T(8,128)S(1)}, f32[256,256]{1,0:T(8,128)S(1)}, u32[]{:S(2)}, u32[]{:S(2)}) collective-permute-start(f32[256,256]{1,0:T(8,128)S(1)} %collective-permute-done.4.refs_9_), channel_id=1, source_target_pairs={{0,1},{1,2},{2,3},{3,4},{4,5},{5,6},{6,7},{7,0},{8,9},{9,10},{10,1... | collective-permute-start | bytes 786440 | tf_op jit(solution)/shard_map/ppermute | solution.py:47
  22.8 11.2 %collective-permute-start.9 = (f32[256,256]{1,0:T(8,128)S(1)}, f32[256,256]{1,0:T(8,128)S(1)}, u32[]{:S(2)}, u32[]{:S(2)}) collective-permute-start(f32[256,256]{1,0:T(8,128)S(1)} %collective-permute-done.8.refs_4_), channel_id=1, source_target_pairs={{0,1},{1,2},{2,3},{3,4},{4,5},{5,6},{6,7},{7,0},{8,9},{9,10},{10,1... | collective-permute-start | bytes 786440 | tf_op jit(solution)/shard_map/ppermute | solution.py:47
  22.8 11.2 %collective-permute-start.12 = (f32[256,256]{1,0:T(8,128)S(1)}, f32[256,256]{1,0:T(8,128)S(1)}, u32[]{:S(2)}, u32[]{:S(2)}) collective-permute-start(f32[256,256]{1,0:T(8,128)S(1)} %collective-permute-done.11.refs_6_), channel_id=1, source_target_pairs={{0,7},{1,0},{2,1},{3,2},{4,3},{5,4},{6,5},{7,6},{8,15},{9,8},{10,9... | collective-permute-start | bytes 786440 | tf_op jit(solution)/shard_map/ppermute | solution.py:47
  26.0 11.2 %collective-permute-start.2 = (f32[256,256]{1,0:T(8,128)S(1)}, f32[256,256]{1,0:T(8,128)S(1)}, u32[]{:S(2)}, u32[]{:S(2)}) collective-permute-start(f32[256,256]{1,0:T(8,128)S(1)} %collective-permute-done.1.refs_2_), channel_id=1, source_target_pairs={{0,7},{1,0},{2,1},{3,2},{4,3},{5,4},{6,5},{7,6},{8,15},{9,8},{10,9... | collective-permute-start | bytes 786440 | tf_op jit(solution)/shard_map/ppermute | solution.py:47
  28.4 11.2 %collective-permute-start.6 = (f32[256,256]{1,0:T(8,128)S(1)}, f32[256,256]{1,0:T(8,128)S(1)}, u32[]{:S(2)}, u32[]{:S(2)}) collective-permute-start(f32[256,256]{1,0:T(8,128)S(1)} %collective-permute-done.5.refs_8_), channel_id=1, source_target_pairs={{0,1},{1,2},{2,3},{3,4},{4,5},{5,6},{6,7},{7,0},{8,9},{9,10},{10,1... | collective-permute-start | bytes 786440 | tf_op jit(solution)/shard_map/ppermute | solution.py:47
  34.0 11.7 %collective-permute-start.10 = (f32[256,256]{1,0:T(8,128)S(1)}, f32[256,256]{1,0:T(8,128)S(1)}, u32[]{:S(2)}, u32[]{:S(2)}) collective-permute-start(f32[256,256]{1,0:T(8,128)S(1)} %collective-permute-done.9.refs_3_), channel_id=1, source_target_pairs={{0,1},{1,2},{2,3},{3,4},{4,5},{5,6},{6,7},{7,0},{8,9},{9,10},{10,1... | collective-permute-start | bytes 786440 | tf_op jit(solution)/shard_map/ppermute | solution.py:47
  34.0 11.8 %collective-permute-start.13 = (f32[256,256]{1,0:T(8,128)S(1)}, f32[256,256]{1,0:T(8,128)}, u32[]{:S(2)}, u32[]{:S(2)}) collective-permute-start(f32[256,256]{1,0:T(8,128)S(1)} %collective-permute-done.12.refs_7_), channel_id=1, source_target_pairs={{0,7},{1,0},{2,1},{3,2},{4,3},{5,4},{6,5},{7,6},{8,15},{9,8},{10,9... | collective-permute-start | bytes 786440 | tf_op jit(solution)/shard_map/ppermute | solution.py:47
  37.3 11.5 %collective-permute-start.3 = (f32[256,256]{1,0:T(8,128)S(1)}, f32[256,256]{1,0:T(8,128)S(1)}, u32[]{:S(2)}, u32[]{:S(2)}) collective-permute-start(f32[256,256]{1,0:T(8,128)S(1)} %collective-permute-done.2.refs_0_), channel_id=1, source_target_pairs={{0,7},{1,0},{2,1},{3,2},{4,3},{5,4},{6,5},{7,6},{8,15},{9,8},{10,9... | collective-permute-start | bytes 786440 | tf_op jit(solution)/shard_map/ppermute | solution.py:47
  39.6 9.8 %collective-permute-start.7 = (f32[256,256]{1,0:T(8,128)S(1)}, f32[256,256]{1,0:T(8,128)S(1)}, u32[]{:S(2)}, u32[]{:S(2)}) collective-permute-start(f32[256,256]{1,0:T(8,128)S(1)} %collective-permute-done.6.refs_3_), channel_id=1, source_target_pairs={{0,1},{1,2},{2,3},{3,4},{4,5},{5,6},{6,7},{7,0},{8,9},{9,10},{10,1... | collective-permute-start | bytes 786440 | tf_op jit(solution)/shard_map/ppermute | solution.py:47
  52.0 6.6 %collective-permute-start.15 = (f32[128,256]{1,0:T(8,128)S(1)}, f32[128,256]{1,0:T(8,128)S(1)}, u32[]{:S(2)}, u32[]{:S(2)}) collective-permute-start(f32[128,256]{1,0:T(8,128)S(1)} %select_add_fusion.1), channel_id=1, source_target_pairs={{0,128},{8,40},{16,144},{24,56},{32,160},{40,8},{48,176},{56,24},{... | collective-permute-start | bytes 393224 | tf_op jit(solution)/shard_map/ppermute | solution.py:40
  61.8 6.6 %collective-permute-start.18 = (f32[128,256]{1,0:T(8,128)S(1)}, f32[128,256]{1,0:T(8,128)S(1)}, u32[]{:S(2)}, u32[]{:S(2)}) collective-permute-start(f32[128,256]{1,0:T(8,128)S(1)} %add_add_fusion.5), channel_id=1, source_target_pairs={{0,32},{8,136},{16,48},{24,152},{32,0},{40,168},{48,16},{56,184},{... | collective-permute-start | bytes 393224 | tf_op jit(solution)/shard_map/ppermute | solution.py:40
  81.4 6.6 %collective-permute-start.23 = (f32[128,256]{1,0:T(8,128)S(1)}, f32[128,256]{1,0:T(8,128)S(1)}, u32[]{:S(2)}, u32[]{:S(2)}) collective-permute-start(f32[128,256]{1,0:T(8,128)S(1)} %select_add_fusion), channel_id=1, source_target_pairs={{0,128},{8,40},{16,144},{24,56},{32,160},{40,8},{48,176},{56,24},{... | collective-permute-start | bytes 393224 | tf_op jit(solution)/shard_map/ppermute | solution.py:40
  89.4 6.6 %collective-permute-start.26 = (f32[128,256]{1,0:T(8,128)S(1)}, f32[128,256]{1,0:T(8,128)S(1)}, u32[]{:S(2)}, u32[]{:S(2)}) collective-permute-start(f32[128,256]{1,0:T(8,128)S(1)} %add_add_fusion.3), channel_id=1, source_target_pairs={{0,32},{8,136},{16,48},{24,152},{32,0},{40,168},{48,16},{56,184},{... | collective-permute-start | bytes 393224 | tf_op jit(solution)/shard_map/ppermute | solution.py:40
  101.1 8.5 %collective-permute-start.40 = (f32[256,256]{1,0:T(8,128)S(1)}, f32[256,256]{1,0:T(8,128)S(1)}, u32[]{:S(2)}, u32[]{:S(2)}) collective-permute-start(f32[256,256]{1,0:T(8,128)S(1)} %get-tuple-element.71), channel_id=1, source_target_pairs={{0,7},{1,0},{2,1},{3,2},{4,3},{5,4},{6,5},{7,6},{8,15},{9,8},{10,9... | collective-permute-start | bytes 786440 | tf_op jit(solution)/shard_map/ppermute | solution.py:47
  103.7 10.4 %collective-permute-start.35 = (f32[256,256]{1,0:T(8,128)S(1)}, f32[256,256]{1,0:T(8,128)S(1)}, u32[]{:S(2)}, u32[]{:S(2)}) collective-permute-start(f32[256,256]{1,0:T(8,128)S(1)} %get-tuple-element.65), channel_id=1, source_target_pairs={{0,1},{1,2},{2,3},{3,4},{4,5},{5,6},{6,7},{7,0},{8,9},{9,10},{10,1... | collective-permute-start | bytes 786440 | tf_op jit(solution)/shard_map/ppermute | solution.py:47
  103.7 16.0 %collective-permute-start.30 = (f32[256,256]{1,0:T(8,128)S(1)}, f32[256,256]{1,0:T(8,128)S(1)}, u32[]{:S(2)}, u32[]{:S(2)}) collective-permute-start(f32[256,256]{1,0:T(8,128)S(1)} %get-tuple-element.53), channel_id=1, source_target_pairs={{0,1},{1,2},{2,3},{3,4},{4,5},{5,6},{6,7},{7,0},{8,9},{9,10},{10,1... | collective-permute-start | bytes 786440 | tf_op jit(solution)/shard_map/ppermute | solution.py:47
  109.6 10.5 %collective-permute-start.41 = (f32[256,256]{1,0:T(8,128)S(1)}, f32[256,256]{1,0:T(8,128)S(1)}, u32[]{:S(2)}, u32[]{:S(2)}) collective-permute-start(f32[256,256]{1,0:T(8,128)S(1)} %add.114), channel_id=1, source_target_pairs={{0,7},{1,0},{2,1},{3,2},{4,3},{5,4},{6,5},{7,6},{8,15},{9,8},{10,9... | collective-permute-start | bytes 786440 | tf_op jit(solution)/shard_map/ppermute | solution.py:47
  113.4 12.3 %collective-permute-start.32 = (f32[256,256]{1,0:T(8,128)S(1)}, f32[256,256]{1,0:T(8,128)S(1)}, u32[]{:S(2)}, u32[]{:S(2)}) collective-permute-start(f32[256,256]{1,0:T(8,128)S(1)} %get-tuple-element.62), channel_id=1, source_target_pairs={{0,7},{1,0},{2,1},{3,2},{4,3},{5,4},{6,5},{7,6},{8,15},{9,8},{10,9... | collective-permute-start | bytes 786440 | tf_op jit(solution)/shard_map/ppermute | solution.py:47
  114.1 15.4 %collective-permute-start.36 = (f32[256,256]{1,0:T(8,128)S(1)}, f32[256,256]{1,0:T(8,128)S(1)}, u32[]{:S(2)}, u32[]{:S(2)}) collective-permute-start(f32[256,256]{1,0:T(8,128)S(1)} %add.109), channel_id=1, source_target_pairs={{0,1},{1,2},{2,3},{3,4},{4,5},{5,6},{6,7},{7,0},{8,9},{9,10},{10,1... | collective-permute-start | bytes 786440 | tf_op jit(solution)/shard_map/ppermute | solution.py:47
  119.8 14.1 %collective-permute-start.31 = (f32[256,256]{1,0:T(8,128)S(1)}, f32[256,256]{1,0:T(8,128)S(1)}, u32[]{:S(2)}, u32[]{:S(2)}) collective-permute-start(f32[256,256]{1,0:T(8,128)S(1)} %add.104), channel_id=1, source_target_pairs={{0,1},{1,2},{2,3},{3,4},{4,5},{5,6},{6,7},{7,0},{8,9},{9,10},{10,1... | collective-permute-start | bytes 786440 | tf_op jit(solution)/shard_map/ppermute | solution.py:47
  120.1 13.9 %collective-permute-start.42 = (f32[256,256]{1,0:T(8,128)S(1)}, f32[256,256]{1,0:T(8,128)S(1)}, u32[]{:S(2)}, u32[]{:S(2)}) collective-permute-start(f32[256,256]{1,0:T(8,128)S(1)} %add.115), channel_id=1, source_target_pairs={{0,7},{1,0},{2,1},{3,2},{4,3},{5,4},{6,5},{7,6},{8,15},{9,8},{10,9... | collective-permute-start | bytes 786440 | tf_op jit(solution)/shard_map/ppermute | solution.py:47
  125.7 11.6 %collective-permute-start.33 = (f32[256,256]{1,0:T(8,128)S(1)}, f32[256,256]{1,0:T(8,128)S(1)}, u32[]{:S(2)}, u32[]{:S(2)}) collective-permute-start(f32[256,256]{1,0:T(8,128)S(1)} %add.106), channel_id=1, source_target_pairs={{0,7},{1,0},{2,1},{3,2},{4,3},{5,4},{6,5},{7,6},{8,15},{9,8},{10,9... | collective-permute-start | bytes 786440 | tf_op jit(solution)/shard_map/ppermute | solution.py:47
  129.5 11.1 %collective-permute-start.37 = (f32[256,256]{1,0:T(8,128)S(1)}, f32[256,256]{1,0:T(8,128)S(1)}, u32[]{:S(2)}, u32[]{:S(2)}) collective-permute-start(f32[256,256]{1,0:T(8,128)S(1)} %add.110), channel_id=1, source_target_pairs={{0,1},{1,2},{2,3},{3,4},{4,5},{5,6},{6,7},{7,0},{8,9},{9,10},{10,1... | collective-permute-start | bytes 786440 | tf_op jit(solution)/shard_map/ppermute | solution.py:47
  133.9 10.4 %collective-permute-start.39 = (f32[256,256]{1,0:T(8,128)S(1)}, f32[256,256]{1,0:T(8,128)S(1)}, u32[]{:S(2)}, u32[]{:S(2)}) collective-permute-start(f32[256,256]{1,0:T(8,128)S(1)} %add.105), channel_id=1, source_target_pairs={{0,1},{1,2},{2,3},{3,4},{4,5},{5,6},{6,7},{7,0},{8,9},{9,10},{10,1... | collective-permute-start | bytes 786440 | tf_op jit(solution)/shard_map/ppermute | solution.py:47
  134.1 10.2 %collective-permute-start.43 = (f32[256,256]{1,0:T(8,128)S(1)}, f32[256,256]{1,0:T(8,128)S(1)}, u32[]{:S(2)}, u32[]{:S(2)}) collective-permute-start(f32[256,256]{1,0:T(8,128)S(1)} %add.116), channel_id=1, source_target_pairs={{0,7},{1,0},{2,1},{3,2},{4,3},{5,4},{6,5},{7,6},{8,15},{9,8},{10,9... | collective-permute-start | bytes 786440 | tf_op jit(solution)/shard_map/ppermute | solution.py:47
  137.4 9.1 %collective-permute-start.34 = (f32[256,256]{1,0:T(8,128)S(1)}, f32[256,256]{1,0:T(8,128)S(1)}, u32[]{:S(2)}, u32[]{:S(2)}) collective-permute-start(f32[256,256]{1,0:T(8,128)S(1)} %add.107), channel_id=1, source_target_pairs={{0,7},{1,0},{2,1},{3,2},{4,3},{5,4},{6,5},{7,6},{8,15},{9,8},{10,9... | collective-permute-start | bytes 786440 | tf_op jit(solution)/shard_map/ppermute | solution.py:47
  140.7 7.7 %collective-permute-start.38 = (f32[256,256]{1,0:T(8,128)S(1)}, f32[256,256]{1,0:T(8,128)S(1)}, u32[]{:S(2)}, u32[]{:S(2)}) collective-permute-start(f32[256,256]{1,0:T(8,128)S(1)} %add.111), channel_id=1, source_target_pairs={{0,1},{1,2},{2,3},{3,4},{4,5},{5,6},{6,7},{7,0},{8,9},{9,10},{10,1... | collective-permute-start | bytes 786440 | tf_op jit(solution)/shard_map/ppermute | solution.py:47
  (31 other events, 297.1 us)
where the time goes:
time: 149 us
  starting transfers between devices  62.9 us (42%)
  waiting for transfers between devices  54.2 us (36%)
  Pallas kernels  25.6 us (17%)
  local copies, waits for them, and re-layouts  3.22 us (2%)
  other arithmetic  2.11 us (1%)
    ppermute x28, starting transfers between devices, shift(): return lax.ppermute(x, 'head', perm)  44.9 us
    ppermute x28, waiting for transfers between devices, shift(): return lax.ppermute(x, 'head', perm)  29.8 us
    ppermute x12, waiting for transfers between devices, sum_over_seq(): one, two, three = (lax.ppermute(mine, 'seq', ring[k]) for k in (1, 2, 3))  19.2 us
    ppermute x12, starting transfers between devices, sum_over_seq(): one, two, three = (lax.ppermute(mine, 'seq', ring[k]) for k in (1, 2, 3))  17.1 us
    pallas_call x2, Pallas kernels, products_of(): pl.pallas_call(grads_body, out_shape=jax.ShapeDtypeStruct((stack.shape[0]...  8.43 us
    pallas_call x1, Pallas kernels, middle(): pl.pallas_call(functools.partial(middle_body, scale), grid=(count // tile...  7.07 us
    pallas_call x3, Pallas kernels, partial(): pl.pallas_call(functools.partial(partial_body, n, distances), out_shape=(...  6.7 us
    pallas_call x2, Pallas kernels, run(): return kernel(z, *operands)  3.4 us
  transfers between devices with their start and end apart: 44, of which 25 were waited for; matrix products, arithmetic and copies ran while one was open for 1% of the time, Pallas kernels for 11%

commit v1 on v0

--- a/solution.py
+++ b/solution.py
@@ -87,9 +87,7 @@
             done.append(work)
             e_down = shift(e_down, down)
             f_up = shift(f_up, up)
-    grad_e = (terms_e[0] + e_down) + e_up
-    grad_f = (terms_f[0] + f_up) + f_down
-    return grad_e, grad_f, done
+    return (terms_e[0], e_down, e_up), (terms_f[0], f_up, f_down), done
 
 
 def two(x):
@@ -337,6 +335,15 @@
     *outs, e_now, f_now = refs
     block = outs[0].shape[0]
     count = len(e_at)
+    if count == 2:
+        for at, rows, grads, to in (
+            (e_at, keys, gpk, outs[:count]),
+            (f_at, values, gpv, outs[count:]),
+        ):
+            for d, ref in zip(at, to):
+                start = pl.multiple_of(lax.rem(z_ref[0] + d, n) * block, block)
+                ref[...] = term_of(rows[pl.ds(start, block), :], grads[...])
+        return
 
     def step(i, carry):
         e_d, f_d = jnp.int32(0), jnp.int32(0)
@@ -385,6 +392,31 @@
         ),
         cost_estimate=pl.CostEstimate(flops=10**9, bytes_accessed=2**22, transcendentals=0),
     )(z, stack, grads)
+
+
+def add_body(a, b, c, d, e, f, out_ref, other_ref):
+    rows = 64
+
+    def step(i, carry):
+        at = pl.ds(pl.multiple_of(i * rows, rows), rows)
+        out_ref[at, :] = (a[at, :] + b[at, :]) + c[at, :]
+        other_ref[at, :] = (d[at, :] + e[at, :]) + f[at, :]
+        return carry
+
+    lax.fori_loop(0, out_ref.shape[0] // rows, step, 0)
+
+
+def add_both(first, second):
+    square = jax.ShapeDtypeStruct(first[0].shape, F32)
+    return pl.pallas_call(
+        add_body,
+        out_shape=(square, square),
+        in_specs=[VMEM] * 6,
+        out_specs=(VMEM, VMEM),
+        compiler_params=pltpu.CompilerParams(vmem_limit_bytes=LIMIT),
+        cost_estimate=pl.CostEstimate(flops=2**18, bytes_accessed=2**21, transcendentals=0),
+        name="add_both",
+    )(*first, *second)
 
 
 def whole(queries, keys, values, proj_e, proj_f, grad_out):
@@ -427,10 +459,11 @@
             terms_e[d] = blocks[i]
         for i, d in enumerate(f_at):
             terms_f[d] = blocks[len(e_at) + i]
-    grad_e, grad_f, (grad_key, grad_value) = scatter_blocks(
+    parts_e, parts_f, (grad_key, grad_value) = scatter_blocks(
         terms_e, terms_f, n,
         [lambda: products_of(z, e_stack, gpk, n), lambda: products_of(z, f_stack, gpv, n)],
     )
+    grad_e, grad_f = add_both(parts_e, parts_f)
     return grad_query, grad_key, grad_value, grad_e, grad_f
 
 

time: 149 us -> 147 us (0.987)
  waiting for transfers between devices: 54.2 us -> 52.3 us
  other arithmetic: 2.11 us -> 0.61 us
    ppermute x28, waiting for transfers between devices: 29.8 us -> 27.8 us  [shift(): return lax.ppermute(x, 'head', perm)]
    add x2 -> x0, other arithmetic: 1.51 us -> none  [the longest x1 0.75 us: scatter_blocks(): grad_f = terms_f[0] + f_up + f_down]
  transfers between devices with their start and end apart: 44 -> 44, of which waited for: 25 -> 23; matrix products, arithmetic and copies ran while one was open for 1% -> 0% of each run, Pallas kernels for 11% -> 11%
where the time goes in v1:
time: 147 us
  starting transfers between devices  63.9 us (43%)
  waiting for transfers between devices  52.3 us (36%)
  Pallas kernels  26.1 us (18%)
  local copies, waits for them, and re-layouts  3.22 us (2%)
    ppermute x28, starting transfers between devices, shift(): return lax.ppermute(x, 'head', perm)  45.9 us
    ppermute x28, waiting for transfers between devices, shift(): return lax.ppermute(x, 'head', perm)  27.8 us
    ppermute x12, waiting for transfers between devices, sum_over_seq(): one, two, three = (lax.ppermute(mine, 'seq', ring[k]) for k in (1, 2, 3))  19.2 us
    ppermute x12, starting transfers between devices, sum_over_seq(): one, two, three = (lax.ppermute(mine, 'seq', ring[k]) for k in (1, 2, 3))  17.1 us
    pallas_call x2, Pallas kernels, products_of(): pl.pallas_call(grads_body, out_shape=jax.ShapeDtypeStruct((stack.shape[0]...  8.45 us
    pallas_call x1, Pallas kernels, middle(): pl.pallas_call(functools.partial(middle_body, scale), grid=(count // tile...  7.08 us
    pallas_call x3, Pallas kernels, partial(): pl.pallas_call(functools.partial(partial_body, n, distances), out_shape=(...  6.69 us
    unnamed x38, local copies, waits for them, and re-layouts  3.22 us
  transfers between devices with their start and end apart: 44, of which 23 were waited for; matrix products, arithmetic and copies ran while one was open for 0% of the time, Pallas kernels for 11%

profile of v1, /device:TPU:6, one launch (start us, length us, event | category | flops | bytes accessed | tf_op | source)
XLA Modules:
  0.0 147.2 jit_solution(6657586574862688410)
XLA Ops:
  0.6 5.9 %collective-permute-start = (f32[256,256]{1,0:T(8,128)}, f32[256,256]{1,0:T(8,128)S(1)}, u32[]{:S(2)}, u32[]{:S(2)}) collective-permute-start(f32[256,256]{1,0:T(8,128)} %refs_0_.1), channel_id=1, source_target_pairs={{0,7},{1,0},{2,1},{3,2},{4,3},{5,4},{6,5},{7,6},{8,15},{9,8},{10,9... | collective-permute-start | bytes 786440 | tf_op jit(solution)/shard_map/ppermute | solution.py:47
  6.6 3.3 %collective-permute-start.11 = (f32[256,256]{1,0:T(8,128)}, f32[256,256]{1,0:T(8,128)S(1)}, u32[]{:S(2)}, u32[]{:S(2)}) collective-permute-start(f32[256,256]{1,0:T(8,128)} %refs_5_.2), channel_id=1, source_target_pairs={{0,7},{1,0},{2,1},{3,2},{4,3},{5,4},{6,5},{7,6},{8,15},{9,8},{10,9... | collective-permute-start | bytes 786440 | tf_op jit(solution)/shard_map/ppermute | solution.py:47
  9.8 3.7 %collective-permute-done.refs_1_ = f32[256,256]{1,0:T(8,128)S(1)} collective-permute-done((f32[256,256]{1,0:T(8,128)}, f32[256,256]{1,0:T(8,128)S(1)}, u32[]{:S(2)}, u32[]{:S(2)}) %collective-permute-start) | collective-permute-done | bytes 262176 | tf_op jit(solution)/shard_map/ppermute | solution.py:47
  13.6 3.6 %collective-permute-start.1 = (f32[256,256]{1,0:T(8,128)S(1)}, f32[256,256]{1,0:T(8,128)S(1)}, u32[]{:S(2)}, u32[]{:S(2)}) collective-permute-start(f32[256,256]{1,0:T(8,128)S(1)} %collective-permute-done.refs_1_), channel_id=1, source_target_pairs={{0,7},{1,0},{2,1},{3,2},{4,3},{5,4},{6,5},{7,6},{8,15},{9,8},{10,9... | collective-permute-start | bytes 786440 | tf_op jit(solution)/shard_map/ppermute | solution.py:47
  17.2 5.6 %collective-permute-done.8.refs_4_ = f32[256,256]{1,0:T(8,128)S(1)} collective-permute-done((f32[256,256]{1,0:T(8,128)}, f32[256,256]{1,0:T(8,128)S(1)}, u32[]{:S(2)}, u32[]{:S(2)}) %collective-permute-start.8) | collective-permute-done | bytes 262176 | tf_op jit(solution)/shard_map/ppermute | solution.py:47
  22.8 3.2 %collective-permute-start.12 = (f32[256,256]{1,0:T(8,128)S(1)}, f32[256,256]{1,0:T(8,128)S(1)}, u32[]{:S(2)}, u32[]{:S(2)}) collective-permute-start(f32[256,256]{1,0:T(8,128)S(1)} %collective-permute-done.11.refs_6_), channel_id=1, source_target_pairs={{0,7},{1,0},{2,1},{3,2},{4,3},{5,4},{6,5},{7,6},{8,15},{9,8},{10,9... | collective-permute-start | bytes 786440 | tf_op jit(solution)/shard_map/ppermute | solution.py:47
  28.4 5.6 %collective-permute-done.9.refs_3_ = f32[256,256]{1,0:T(8,128)S(1)} collective-permute-done((f32[256,256]{1,0:T(8,128)S(1)}, f32[256,256]{1,0:T(8,128)S(1)}, u32[]{:S(2)}, u32[]{:S(2)}) %collective-permute-start.9) | collective-permute-done | bytes 262176 | tf_op jit(solution)/shard_map/ppermute | solution.py:47
  34.0 3.2 %collective-permute-start.13 = (f32[256,256]{1,0:T(8,128)S(1)}, f32[256,256]{1,0:T(8,128)}, u32[]{:S(2)}, u32[]{:S(2)}) collective-permute-start(f32[256,256]{1,0:T(8,128)S(1)} %collective-permute-done.12.refs_7_), channel_id=1, source_target_pairs={{0,7},{1,0},{2,1},{3,2},{4,3},{5,4},{6,5},{7,6},{8,15},{9,8},{10,9... | collective-permute-start | bytes 786440 | tf_op jit(solution)/shard_map/ppermute | solution.py:47
  42.2 3.5 %shard_map.101 = (f32[128,256]{1,0:T(8,128)S(1)}, f32[128,256]{1,0:T(8,128)S(1)}, f32[2048,256]{1,0:T(8,128)}, f32[2048,256]{1,0:T(8,128)}) custom-call(s32[1]{0:T(128)} %bitcast.z_ref.refs_0_, f32[256,256]{1,0:T(8,128)} %refs_0_.1, f32[256,256]{1,0:T(8,128)} %copy-done.8, f32[256,256]{1,0:T(8,128)} %copy-done.12, f32[256,256]{1,0:T(8,128)} %copy-done.16, ...), custom_call_target="tpu_custom_call" | custom-call | flops 500000000 | bytes 5242880 | tf_op jit(solution)/shard_map/pallas_call | solution.py:219
  46.5 2.3 %shard_map.102 = (f32[128,256]{1,0:T(8,128)S(1)}, f32[128,256]{1,0:T(8,128)S(1)}, f32[2048,256]{1,0:T(8,128)}, f32[2048,256]{1,0:T(8,128)}) custom-call(s32[1]{0:T(128)} %bitcast.z_ref.refs_0_, f32[256,256]{1,0:T(8,128)} %copy-done.14, f32[256,256]{1,0:T(8,128)} %copy-done.18, ...), custom_call_target="tpu_custom_call", output_to_operand_aliasing={{2}: (9, {}), {3}: (10, {})} | custom-call | flops 200000000 | bytes 2097152 | tf_op jit(solution)/shard_map/pallas_call | solution.py:219
  53.5 2.1 %collective-permute-start.16 = (f32[128,256]{1,0:T(8,128)S(1)}, f32[128,256]{1,0:T(8,128)S(1)}, u32[]{:S(2)}, u32[]{:S(2)}) collective-permute-start(f32[128,256]{1,0:T(8,128)S(1)} %select_add_fusion.1), channel_id=1, source_target_pairs={{0,64},{8,24},{16,80},{24,40},{32,96},{40,56},{48,112},{56,8},{64,... | collective-permute-start | bytes 393224 | tf_op jit(solution)/shard_map/ppermute | solution.py:40
  55.6 3.0 %collective-permute-done.15 = f32[128,256]{1,0:T(8,128)S(1)} collective-permute-done((f32[128,256]{1,0:T(8,128)S(1)}, f32[128,256]{1,0:T(8,128)S(1)}, u32[]{:S(2)}, u32[]{:S(2)}) %collective-permute-start.15) | collective-permute-done | bytes 131104 | tf_op jit(solution)/shard_map/ppermute | solution.py:40
  58.6 3.2 %collective-permute-done.17 = f32[128,256]{1,0:T(8,128)S(1)} collective-permute-done((f32[128,256]{1,0:T(8,128)S(1)}, f32[128,256]{1,0:T(8,128)S(1)}, u32[]{:S(2)}, u32[]{:S(2)}) %collective-permute-start.17) | collective-permute-done | bytes 131104 | tf_op jit(solution)/shard_map/ppermute | solution.py:40
  61.8 3.3 %collective-permute-start.18 = (f32[128,256]{1,0:T(8,128)S(1)}, f32[128,256]{1,0:T(8,128)S(1)}, u32[]{:S(2)}, u32[]{:S(2)}) collective-permute-start(f32[128,256]{1,0:T(8,128)S(1)} %add_add_fusion.3), channel_id=1, source_target_pairs={{0,32},{8,136},{16,48},{24,152},{32,0},{40,168},{48,16},{56,184},{... | collective-permute-start | bytes 393224 | tf_op jit(solution)/shard_map/ppermute | solution.py:40
  65.8 2.6 %collective-permute-start.20 = (f32[128,256]{1,0:T(8,128)S(1)}, f32[128,256]{1,0:T(8,128)S(1)}, u32[]{:S(2)}, u32[]{:S(2)}) collective-permute-start(f32[128,256]{1,0:T(8,128)S(1)} %add_add_fusion.3), channel_id=1, source_target_pairs={{0,48},{8,200},{16,0},{24,216},{32,16},{40,232},{48,32},{56,248},{... | collective-permute-start | bytes 393224 | tf_op jit(solution)/shard_map/ppermute | solution.py:40
  68.4 2.9 %collective-permute-done.19 = f32[128,256]{1,0:T(8,128)S(1)} collective-permute-done((f32[128,256]{1,0:T(8,128)S(1)}, f32[128,256]{1,0:T(8,128)S(1)}, u32[]{:S(2)}, u32[]{:S(2)}) %collective-permute-start.19) | collective-permute-done | bytes 131104 | tf_op jit(solution)/shard_map/ppermute | solution.py:40
  72.8 7.1 %middle.1 = (f32[2048,128]{1,0:T(8,128)}, f32[128,256]{1,0:T(8,128)S(1)}, f32[128,256]{1,0:T(8,128)S(1)}) custom-call(f32[2048,128]{1,0:T(8,128)S(1)} %copy-done.6, f32[2048,128]{1,0:T(8,128)S(1)} %copy-done.7, f32[128,256]{1,0:T(8,128)S(1)} %get-tuple-element.82.pk_ref, f32[128,256]{1,0:T(8,128)S(1)} %get-tuple-element.81.pv_ref), custom_call_target="tpu_custom_call" | custom-call | flops 10000000000 | bytes 4194304 | tf_op jit(solution)/shard_map/middle/pallas_call | solution.py:307
  83.6 4.4 %collective-permute-done.23 = f32[128,256]{1,0:T(8,128)S(1)} collective-permute-done((f32[128,256]{1,0:T(8,128)S(1)}, f32[128,256]{1,0:T(8,128)S(1)}, u32[]{:S(2)}, u32[]{:S(2)}) %collective-permute-start.23) | collective-permute-done | bytes 131104 | tf_op jit(solution)/shard_map/ppermute | solution.py:40
  90.9 2.6 %collective-permute-start.27 = (f32[128,256]{1,0:T(8,128)S(1)}, f32[128,256]{1,0:T(8,128)S(1)}, u32[]{:S(2)}, u32[]{:S(2)}) collective-permute-start(f32[128,256]{1,0:T(8,128)S(1)} %add_add_fusion.1), channel_id=1, source_target_pairs={{0,16},{8,72},{16,32},{24,88},{32,48},{40,104},{48,0},{56,120},{64... | collective-permute-start | bytes 393224 | tf_op jit(solution)/shard_map/ppermute | solution.py:40
  100.7 2.6 %collective-permute-start.40 = (f32[256,256]{1,0:T(8,128)S(1)}, f32[256,256]{1,0:T(8,128)S(1)}, u32[]{:S(2)}, u32[]{:S(2)}) collective-permute-start(f32[256,256]{1,0:T(8,128)S(1)} %get-tuple-element.73), channel_id=1, source_target_pairs={{0,7},{1,0},{2,1},{3,2},{4,3},{5,4},{6,5},{7,6},{8,15},{9,8},{10,9... | collective-permute-start | bytes 786440 | tf_op jit(solution)/shard_map/ppermute | solution.py:47
  103.3 3.2 %collective-permute-start.32 = (f32[256,256]{1,0:T(8,128)S(1)}, f32[256,256]{1,0:T(8,128)S(1)}, u32[]{:S(2)}, u32[]{:S(2)}) collective-permute-start(f32[256,256]{1,0:T(8,128)S(1)} %get-tuple-element.64), channel_id=1, source_target_pairs={{0,7},{1,0},{2,1},{3,2},{4,3},{5,4},{6,5},{7,6},{8,15},{9,8},{10,9... | collective-permute-start | bytes 786440 | tf_op jit(solution)/shard_map/ppermute | solution.py:47
  106.5 2.6 %shard_map.105 = (f32[256,256]{1,0:T(8,128)S(1)}, f32[256,256]{1,0:T(8,128)S(1)}, f32[256,256]{1,0:T(8,128)S(1)}, f32[256,256]{1,0:T(8,128)S(1)}, f32[256,256]{1...) custom-call(s32[1]{0:T(128)} %bitcast.z_ref.refs_0_, ...), custom_call_target="tpu_custom_call" | custom-call | flops 1000000000 | bytes 4194304 | tf_op jit(solution)/shard_map/pallas_call | solution.py:433
  110.0 3.8 %collective-permute-start.41 = (f32[256,256]{1,0:T(8,128)S(1)}, f32[256,256]{1,0:T(8,128)S(1)}, u32[]{:S(2)}, u32[]{:S(2)}) collective-permute-start(f32[256,256]{1,0:T(8,128)S(1)} %add.99), channel_id=1, source_target_pairs={{0,7},{1,0},{2,1},{3,2},{4,3},{5,4},{6,5},{7,6},{8,15},{9,8},{10,9... | collective-permute-start | bytes 786440 | tf_op jit(solution)/shard_map/ppermute | solution.py:47
  113.9 4.2 %shard_map.106 = f32[2048,128]{1,0:T(8,128)} custom-call(s32[1]{0:T(128)} %bitcast.z_ref.refs_0_, f32[2048,256]{1,0:T(8,128)S(1)} %copy-done.4, f32[128,256]{1,0:T(8,128)S(1)} %get-tuple-element.80.refs_3_.grads_ref), custom_call_target="tpu_custom_call" | custom-call | flops 1000000000 | bytes 4194304 | tf_op jit(solution)/shard_map/pallas_call | solution.py:378
  118.2 3.3 %collective-permute-start.33 = (f32[256,256]{1,0:T(8,128)S(1)}, f32[256,256]{1,0:T(8,128)S(1)}, u32[]{:S(2)}, u32[]{:S(2)}) collective-permute-start(f32[256,256]{1,0:T(8,128)S(1)} %add.94), channel_id=1, source_target_pairs={{0,7},{1,0},{2,1},{3,2},{4,3},{5,4},{6,5},{7,6},{8,15},{9,8},{10,9... | collective-permute-start | bytes 786440 | tf_op jit(solution)/shard_map/ppermute | solution.py:47
  121.7 3.4 %collective-permute-start.42 = (f32[256,256]{1,0:T(8,128)S(1)}, f32[256,256]{1,0:T(8,128)S(1)}, u32[]{:S(2)}, u32[]{:S(2)}) collective-permute-start(f32[256,256]{1,0:T(8,128)S(1)} %add.100), channel_id=1, source_target_pairs={{0,7},{1,0},{2,1},{3,2},{4,3},{5,4},{6,5},{7,6},{8,15},{9,8},{10,9... | collective-permute-start | bytes 786440 | tf_op jit(solution)/shard_map/ppermute | solution.py:47
  125.2 4.2 %shard_map.107 = f32[2048,128]{1,0:T(8,128)} custom-call(s32[1]{0:T(128)} %bitcast.z_ref.refs_0_, f32[2048,256]{1,0:T(8,128)S(1)} %copy-done.5, f32[128,256]{1,0:T(8,128)S(1)} %get-tuple-element.79.refs_4_.grads_ref), custom_call_target="tpu_custom_call" | custom-call | flops 1000000000 | bytes 4194304 | tf_op jit(solution)/shard_map/pallas_call | solution.py:378
  129.5 3.3 %collective-permute-start.34 = (f32[256,256]{1,0:T(8,128)S(1)}, f32[256,256]{1,0:T(8,128)S(1)}, u32[]{:S(2)}, u32[]{:S(2)}) collective-permute-start(f32[256,256]{1,0:T(8,128)S(1)} %add.95), channel_id=1, source_target_pairs={{0,7},{1,0},{2,1},{3,2},{4,3},{5,4},{6,5},{7,6},{8,15},{9,8},{10,9... | collective-permute-start | bytes 786440 | tf_op jit(solution)/shard_map/ppermute | solution.py:47
  133.0 3.4 %collective-permute-start.43 = (f32[256,256]{1,0:T(8,128)S(1)}, f32[256,256]{1,0:T(8,128)S(1)}, u32[]{:S(2)}, u32[]{:S(2)}) collective-permute-start(f32[256,256]{1,0:T(8,128)S(1)} %add.101), channel_id=1, source_target_pairs={{0,7},{1,0},{2,1},{3,2},{4,3},{5,4},{6,5},{7,6},{8,15},{9,8},{10,9... | collective-permute-start | bytes 786440 | tf_op jit(solution)/shard_map/ppermute | solution.py:47
  136.5 2.9 %collective-permute-done.34.b = f32[256,256]{1,0:T(8,128)S(1)} collective-permute-done((f32[256,256]{1,0:T(8,128)S(1)}, f32[256,256]{1,0:T(8,128)S(1)}, u32[]{:S(2)}, u32[]{:S(2)}) %collective-permute-start.34) | collective-permute-done | bytes 262176 | tf_op jit(solution)/shard_map/ppermute | solution.py:47
  139.4 3.8 %collective-permute-done.39.e = f32[256,256]{1,0:T(8,128)S(1)} collective-permute-done((f32[256,256]{1,0:T(8,128)S(1)}, f32[256,256]{1,0:T(8,128)S(1)}, u32[]{:S(2)}, u32[]{:S(2)}) %collective-permute-start.39) | collective-permute-done | bytes 262176 | tf_op jit(solution)/shard_map/ppermute | solution.py:47
  143.2 3.1 %collective-permute-done.38.c = f32[256,256]{1,0:T(8,128)S(1)} collective-permute-done((f32[256,256]{1,0:T(8,128)S(1)}, f32[256,256]{1,0:T(8,128)S(1)}, u32[]{:S(2)}, u32[]{:S(2)}) %collective-permute-start.38) | collective-permute-done | bytes 262176 | tf_op jit(solution)/shard_map/ppermute | solution.py:47
  (123 shorter events, 31.3 us)
Async XLA Ops:
  0.6 12.9 %collective-permute-start = (f32[256,256]{1,0:T(8,128)}, f32[256,256]{1,0:T(8,128)S(1)}, u32[]{:S(2)}, u32[]{:S(2)}) collective-permute-start(f32[256,256]{1,0:T(8,128)} %refs_0_.1), channel_id=1, source_target_pairs={{0,7},{1,0},{2,1},{3,2},{4,3},{5,4},{6,5},{7,6},{8,15},{9,8},{10,9... | collective-permute-start | bytes 786440 | tf_op jit(solution)/shard_map/ppermute | solution.py:47
  6.6 10.6 %collective-permute-start.4 = (f32[256,256]{1,0:T(8,128)}, f32[256,256]{1,0:T(8,128)S(1)}, u32[]{:S(2)}, u32[]{:S(2)}) collective-permute-start(f32[256,256]{1,0:T(8,128)} %refs_5_.2), channel_id=1, source_target_pairs={{0,1},{1,2},{2,3},{3,4},{4,5},{5,6},{6,7},{7,0},{8,9},{9,10},{10,1... | collective-permute-start | bytes 786440 | tf_op jit(solution)/shard_map/ppermute | solution.py:47
  6.6 16.2 %collective-permute-start.8 = (f32[256,256]{1,0:T(8,128)}, f32[256,256]{1,0:T(8,128)S(1)}, u32[]{:S(2)}, u32[]{:S(2)}) collective-permute-start(f32[256,256]{1,0:T(8,128)} %refs_0_.1), channel_id=1, source_target_pairs={{0,1},{1,2},{2,3},{3,4},{4,5},{5,6},{6,7},{7,0},{8,9},{9,10},{10,1... | collective-permute-start | bytes 786440 | tf_op jit(solution)/shard_map/ppermute | solution.py:47
  6.6 16.2 %collective-permute-start.11 = (f32[256,256]{1,0:T(8,128)}, f32[256,256]{1,0:T(8,128)S(1)}, u32[]{:S(2)}, u32[]{:S(2)}) collective-permute-start(f32[256,256]{1,0:T(8,128)} %refs_5_.2), channel_id=1, source_target_pairs={{0,7},{1,0},{2,1},{3,2},{4,3},{5,4},{6,5},{7,6},{8,15},{9,8},{10,9... | collective-permute-start | bytes 786440 | tf_op jit(solution)/shard_map/ppermute | solution.py:47
  13.6 12.5 %collective-permute-start.1 = (f32[256,256]{1,0:T(8,128)S(1)}, f32[256,256]{1,0:T(8,128)S(1)}, u32[]{:S(2)}, u32[]{:S(2)}) collective-permute-start(f32[256,256]{1,0:T(8,128)S(1)} %collective-permute-done.refs_1_), channel_id=1, source_target_pairs={{0,7},{1,0},{2,1},{3,2},{4,3},{5,4},{6,5},{7,6},{8,15},{9,8},{10,9... | collective-permute-start | bytes 786440 | tf_op jit(solution)/shard_map/ppermute | solution.py:47
  17.2 11.2 %collective-permute-start.5 = (f32[256,256]{1,0:T(8,128)S(1)}, f32[256,256]{1,0:T(8,128)S(1)}, u32[]{:S(2)}, u32[]{:S(2)}) collective-permute-start(f32[256,256]{1,0:T(8,128)S(1)} %collective-permute-done.4.refs_9_), channel_id=1, source_target_pairs={{0,1},{1,2},{2,3},{3,4},{4,5},{5,6},{6,7},{7,0},{8,9},{9,10},{10,1... | collective-permute-start | bytes 786440 | tf_op jit(solution)/shard_map/ppermute | solution.py:47
  22.8 11.2 %collective-permute-start.9 = (f32[256,256]{1,0:T(8,128)S(1)}, f32[256,256]{1,0:T(8,128)S(1)}, u32[]{:S(2)}, u32[]{:S(2)}) collective-permute-start(f32[256,256]{1,0:T(8,128)S(1)} %collective-permute-done.8.refs_4_), channel_id=1, source_target_pairs={{0,1},{1,2},{2,3},{3,4},{4,5},{5,6},{6,7},{7,0},{8,9},{9,10},{10,1... | collective-permute-start | bytes 786440 | tf_op jit(solution)/shard_map/ppermute | solution.py:47
  22.8 11.2 %collective-permute-start.12 = (f32[256,256]{1,0:T(8,128)S(1)}, f32[256,256]{1,0:T(8,128)S(1)}, u32[]{:S(2)}, u32[]{:S(2)}) collective-permute-start(f32[256,256]{1,0:T(8,128)S(1)} %collective-permute-done.11.refs_6_), channel_id=1, source_target_pairs={{0,7},{1,0},{2,1},{3,2},{4,3},{5,4},{6,5},{7,6},{8,15},{9,8},{10,9... | collective-permute-start | bytes 786440 | tf_op jit(solution)/shard_map/ppermute | solution.py:47
  26.0 11.2 %collective-permute-start.2 = (f32[256,256]{1,0:T(8,128)S(1)}, f32[256,256]{1,0:T(8,128)S(1)}, u32[]{:S(2)}, u32[]{:S(2)}) collective-permute-start(f32[256,256]{1,0:T(8,128)S(1)} %collective-permute-done.1.refs_2_), channel_id=1, source_target_pairs={{0,7},{1,0},{2,1},{3,2},{4,3},{5,4},{6,5},{7,6},{8,15},{9,8},{10,9... | collective-permute-start | bytes 786440 | tf_op jit(solution)/shard_map/ppermute | solution.py:47
  28.4 11.2 %collective-permute-start.6 = (f32[256,256]{1,0:T(8,128)S(1)}, f32[256,256]{1,0:T(8,128)S(1)}, u32[]{:S(2)}, u32[]{:S(2)}) collective-permute-start(f32[256,256]{1,0:T(8,128)S(1)} %collective-permute-done.5.refs_8_), channel_id=1, source_target_pairs={{0,1},{1,2},{2,3},{3,4},{4,5},{5,6},{6,7},{7,0},{8,9},{9,10},{10,1... | collective-permute-start | bytes 786440 | tf_op jit(solution)/shard_map/ppermute | solution.py:47
  34.0 11.7 %collective-permute-start.10 = (f32[256,256]{1,0:T(8,128)S(1)}, f32[256,256]{1,0:T(8,128)S(1)}, u32[]{:S(2)}, u32[]{:S(2)}) collective-permute-start(f32[256,256]{1,0:T(8,128)S(1)} %collective-permute-done.9.refs_3_), channel_id=1, source_target_pairs={{0,1},{1,2},{2,3},{3,4},{4,5},{5,6},{6,7},{7,0},{8,9},{9,10},{10,1... | collective-permute-start | bytes 786440 | tf_op jit(solution)/shard_map/ppermute | solution.py:47
  34.0 11.7 %collective-permute-start.13 = (f32[256,256]{1,0:T(8,128)S(1)}, f32[256,256]{1,0:T(8,128)}, u32[]{:S(2)}, u32[]{:S(2)}) collective-permute-start(f32[256,256]{1,0:T(8,128)S(1)} %collective-permute-done.12.refs_7_), channel_id=1, source_target_pairs={{0,7},{1,0},{2,1},{3,2},{4,3},{5,4},{6,5},{7,6},{8,15},{9,8},{10,9... | collective-permute-start | bytes 786440 | tf_op jit(solution)/shard_map/ppermute | solution.py:47
  37.3 11.5 %collective-permute-start.3 = (f32[256,256]{1,0:T(8,128)S(1)}, f32[256,256]{1,0:T(8,128)S(1)}, u32[]{:S(2)}, u32[]{:S(2)}) collective-permute-start(f32[256,256]{1,0:T(8,128)S(1)} %collective-permute-done.2.refs_0_), channel_id=1, source_target_pairs={{0,7},{1,0},{2,1},{3,2},{4,3},{5,4},{6,5},{7,6},{8,15},{9,8},{10,9... | collective-permute-start | bytes 786440 | tf_op jit(solution)/shard_map/ppermute | solution.py:47
  39.6 9.8 %collective-permute-start.7 = (f32[256,256]{1,0:T(8,128)S(1)}, f32[256,256]{1,0:T(8,128)S(1)}, u32[]{:S(2)}, u32[]{:S(2)}) collective-permute-start(f32[256,256]{1,0:T(8,128)S(1)} %collective-permute-done.6.refs_3_), channel_id=1, source_target_pairs={{0,1},{1,2},{2,3},{3,4},{4,5},{5,6},{6,7},{7,0},{8,9},{9,10},{10,1... | collective-permute-start | bytes 786440 | tf_op jit(solution)/shard_map/ppermute | solution.py:47
  52.0 6.6 %collective-permute-start.15 = (f32[128,256]{1,0:T(8,128)S(1)}, f32[128,256]{1,0:T(8,128)S(1)}, u32[]{:S(2)}, u32[]{:S(2)}) collective-permute-start(f32[128,256]{1,0:T(8,128)S(1)} %select_add_fusion.1), channel_id=1, source_target_pairs={{0,128},{8,40},{16,144},{24,56},{32,160},{40,8},{48,176},{56,24},{... | collective-permute-start | bytes 393224 | tf_op jit(solution)/shard_map/ppermute | solution.py:40
  61.8 6.6 %collective-permute-start.18 = (f32[128,256]{1,0:T(8,128)S(1)}, f32[128,256]{1,0:T(8,128)S(1)}, u32[]{:S(2)}, u32[]{:S(2)}) collective-permute-start(f32[128,256]{1,0:T(8,128)S(1)} %add_add_fusion.3), channel_id=1, source_target_pairs={{0,32},{8,136},{16,48},{24,152},{32,0},{40,168},{48,16},{56,184},{... | collective-permute-start | bytes 393224 | tf_op jit(solution)/shard_map/ppermute | solution.py:40
  81.4 6.6 %collective-permute-start.23 = (f32[128,256]{1,0:T(8,128)S(1)}, f32[128,256]{1,0:T(8,128)S(1)}, u32[]{:S(2)}, u32[]{:S(2)}) collective-permute-start(f32[128,256]{1,0:T(8,128)S(1)} %select_add_fusion), channel_id=1, source_target_pairs={{0,128},{8,40},{16,144},{24,56},{32,160},{40,8},{48,176},{56,24},{... | collective-permute-start | bytes 393224 | tf_op jit(solution)/shard_map/ppermute | solution.py:40
  89.4 6.6 %collective-permute-start.26 = (f32[128,256]{1,0:T(8,128)S(1)}, f32[128,256]{1,0:T(8,128)S(1)}, u32[]{:S(2)}, u32[]{:S(2)}) collective-permute-start(f32[128,256]{1,0:T(8,128)S(1)} %add_add_fusion.1), channel_id=1, source_target_pairs={{0,32},{8,136},{16,48},{24,152},{32,0},{40,168},{48,16},{56,184},{... | collective-permute-start | bytes 393224 | tf_op jit(solution)/shard_map/ppermute | solution.py:40
  100.7 9.3 %collective-permute-start.40 = (f32[256,256]{1,0:T(8,128)S(1)}, f32[256,256]{1,0:T(8,128)S(1)}, u32[]{:S(2)}, u32[]{:S(2)}) collective-permute-start(f32[256,256]{1,0:T(8,128)S(1)} %get-tuple-element.73), channel_id=1, source_target_pairs={{0,7},{1,0},{2,1},{3,2},{4,3},{5,4},{6,5},{7,6},{8,15},{9,8},{10,9... | collective-permute-start | bytes 786440 | tf_op jit(solution)/shard_map/ppermute | solution.py:47
  103.3 10.5 %collective-permute-start.35 = (f32[256,256]{1,0:T(8,128)S(1)}, f32[256,256]{1,0:T(8,128)S(1)}, u32[]{:S(2)}, u32[]{:S(2)}) collective-permute-start(f32[256,256]{1,0:T(8,128)S(1)} %get-tuple-element.67), channel_id=1, source_target_pairs={{0,1},{1,2},{2,3},{3,4},{4,5},{5,6},{6,7},{7,0},{8,9},{9,10},{10,1... | collective-permute-start | bytes 786440 | tf_op jit(solution)/shard_map/ppermute | solution.py:47
  103.3 14.9 %collective-permute-start.32 = (f32[256,256]{1,0:T(8,128)S(1)}, f32[256,256]{1,0:T(8,128)S(1)}, u32[]{:S(2)}, u32[]{:S(2)}) collective-permute-start(f32[256,256]{1,0:T(8,128)S(1)} %get-tuple-element.64), channel_id=1, source_target_pairs={{0,7},{1,0},{2,1},{3,2},{4,3},{5,4},{6,5},{7,6},{8,15},{9,8},{10,9... | collective-permute-start | bytes 786440 | tf_op jit(solution)/shard_map/ppermute | solution.py:47
  106.5 14.9 %collective-permute-start.30 = (f32[256,256]{1,0:T(8,128)S(1)}, f32[256,256]{1,0:T(8,128)S(1)}, u32[]{:S(2)}, u32[]{:S(2)}) collective-permute-start(f32[256,256]{1,0:T(8,128)S(1)} %get-tuple-element.55), channel_id=1, source_target_pairs={{0,1},{1,2},{2,3},{3,4},{4,5},{5,6},{6,7},{7,0},{8,9},{9,10},{10,1... | collective-permute-start | bytes 786440 | tf_op jit(solution)/shard_map/ppermute | solution.py:47
  110.0 11.6 %collective-permute-start.41 = (f32[256,256]{1,0:T(8,128)S(1)}, f32[256,256]{1,0:T(8,128)S(1)}, u32[]{:S(2)}, u32[]{:S(2)}) collective-permute-start(f32[256,256]{1,0:T(8,128)S(1)} %add.99), channel_id=1, source_target_pairs={{0,7},{1,0},{2,1},{3,2},{4,3},{5,4},{6,5},{7,6},{8,15},{9,8},{10,9... | collective-permute-start | bytes 786440 | tf_op jit(solution)/shard_map/ppermute | solution.py:47
  113.8 11.2 %collective-permute-start.36 = (f32[256,256]{1,0:T(8,128)S(1)}, f32[256,256]{1,0:T(8,128)S(1)}, u32[]{:S(2)}, u32[]{:S(2)}) collective-permute-start(f32[256,256]{1,0:T(8,128)S(1)} %add.96), channel_id=1, source_target_pairs={{0,1},{1,2},{2,3},{3,4},{4,5},{5,6},{6,7},{7,0},{8,9},{9,10},{10,1... | collective-permute-start | bytes 786440 | tf_op jit(solution)/shard_map/ppermute | solution.py:47
  118.2 11.2 %collective-permute-start.33 = (f32[256,256]{1,0:T(8,128)S(1)}, f32[256,256]{1,0:T(8,128)S(1)}, u32[]{:S(2)}, u32[]{:S(2)}) collective-permute-start(f32[256,256]{1,0:T(8,128)S(1)} %add.94), channel_id=1, source_target_pairs={{0,7},{1,0},{2,1},{3,2},{4,3},{5,4},{6,5},{7,6},{8,15},{9,8},{10,9... | collective-permute-start | bytes 786440 | tf_op jit(solution)/shard_map/ppermute | solution.py:47
  121.5 11.2 %collective-permute-start.31 = (f32[256,256]{1,0:T(8,128)S(1)}, f32[256,256]{1,0:T(8,128)S(1)}, u32[]{:S(2)}, u32[]{:S(2)}) collective-permute-start(f32[256,256]{1,0:T(8,128)S(1)} %add.92), channel_id=1, source_target_pairs={{0,1},{1,2},{2,3},{3,4},{4,5},{5,6},{6,7},{7,0},{8,9},{9,10},{10,1... | collective-permute-start | bytes 786440 | tf_op jit(solution)/shard_map/ppermute | solution.py:47
  121.7 11.3 %collective-permute-start.42 = (f32[256,256]{1,0:T(8,128)S(1)}, f32[256,256]{1,0:T(8,128)S(1)}, u32[]{:S(2)}, u32[]{:S(2)}) collective-permute-start(f32[256,256]{1,0:T(8,128)S(1)} %add.100), channel_id=1, source_target_pairs={{0,7},{1,0},{2,1},{3,2},{4,3},{5,4},{6,5},{7,6},{8,15},{9,8},{10,9... | collective-permute-start | bytes 786440 | tf_op jit(solution)/shard_map/ppermute | solution.py:47
  125.1 11.3 %collective-permute-start.37 = (f32[256,256]{1,0:T(8,128)S(1)}, f32[256,256]{1,0:T(8,128)S(1)}, u32[]{:S(2)}, u32[]{:S(2)}) collective-permute-start(f32[256,256]{1,0:T(8,128)S(1)} %add.97), channel_id=1, source_target_pairs={{0,1},{1,2},{2,3},{3,4},{4,5},{5,6},{6,7},{7,0},{8,9},{9,10},{10,1... | collective-permute-start | bytes 786440 | tf_op jit(solution)/shard_map/ppermute | solution.py:47
  129.5 10.0 %collective-permute-start.34 = (f32[256,256]{1,0:T(8,128)S(1)}, f32[256,256]{1,0:T(8,128)S(1)}, u32[]{:S(2)}, u32[]{:S(2)}) collective-permute-start(f32[256,256]{1,0:T(8,128)S(1)} %add.95), channel_id=1, source_target_pairs={{0,7},{1,0},{2,1},{3,2},{4,3},{5,4},{6,5},{7,6},{8,15},{9,8},{10,9... | collective-permute-start | bytes 786440 | tf_op jit(solution)/shard_map/ppermute | solution.py:47
  132.8 10.5 %collective-permute-start.39 = (f32[256,256]{1,0:T(8,128)S(1)}, f32[256,256]{1,0:T(8,128)S(1)}, u32[]{:S(2)}, u32[]{:S(2)}) collective-permute-start(f32[256,256]{1,0:T(8,128)S(1)} %add.93), channel_id=1, source_target_pairs={{0,1},{1,2},{2,3},{3,4},{4,5},{5,6},{6,7},{7,0},{8,9},{9,10},{10,1... | collective-permute-start | bytes 786440 | tf_op jit(solution)/shard_map/ppermute | solution.py:47
  133.0 10.3 %collective-permute-start.43 = (f32[256,256]{1,0:T(8,128)S(1)}, f32[256,256]{1,0:T(8,128)S(1)}, u32[]{:S(2)}, u32[]{:S(2)}) collective-permute-start(f32[256,256]{1,0:T(8,128)S(1)} %add.101), channel_id=1, source_target_pairs={{0,7},{1,0},{2,1},{3,2},{4,3},{5,4},{6,5},{7,6},{8,15},{9,8},{10,9... | collective-permute-start | bytes 786440 | tf_op jit(solution)/shard_map/ppermute | solution.py:47
  136.4 9.9 %collective-permute-start.38 = (f32[256,256]{1,0:T(8,128)S(1)}, f32[256,256]{1,0:T(8,128)S(1)}, u32[]{:S(2)}, u32[]{:S(2)}) collective-permute-start(f32[256,256]{1,0:T(8,128)S(1)} %add.98), channel_id=1, source_target_pairs={{0,1},{1,2},{2,3},{3,4},{4,5},{5,6},{6,7},{7,0},{8,9},{9,10},{10,1... | collective-permute-start | bytes 786440 | tf_op jit(solution)/shard_map/ppermute | solution.py:47
  (31 other events, 289.7 us)
